TPU v7x, 512 devices: a whole 4x8x8 slice. The times are simulated.
512 devices in a mesh: row: 16 (over z, core), col: 32 (over y, x).
Axes of the slice: x: 4, y: 8, z: 8, core: 2. Of those that a mesh axis runs over, the one named last changes fastest.
Arguments:
- pivots: int32 [2], replicated, may hold values from 0 to 63, as said below
- demand: float32 [16384, 512], P('row', 'col'), may hold values from -0.09 to 0.09
- prices: float32 [512, 16384], P('row', 'col'), may hold values from -0.09 to 0.09
Outputs:
- reduced: float32 [16384, 16384], P('row', 'col')
Inputs may be any that keep to these rules, and one draw needn't show every extreme that they name: `pivots`: two different panel indices, one of which is the last panel.
All inputs are finite; a program needn't handle non-finite values.
Results may differ from a plain program's by a relative error of at most 0.0003.
Values sent between devices are 32-bit elements; how exact they have to be, the bound alone decides.
No kernel may reach another device: no remote copies, remote signals or barrier semaphores. Data moves between devices by JAX's collectives and lax.ppermute only.
A program may use at most 64 MiB of HBM per device.

v0:
```python
import jax
import jax.numpy as jnp
from jax import lax
from jax.sharding import PartitionSpec as P

PW = 256


def spread(block, axis, holder):
    block = jnp.where(lax.axis_index(axis) == holder, block, jnp.zeros_like(block))
    return lax.psum(block, axis)


def product(left, right):
    return jnp.dot(left, right, precision=lax.Precision.HIGHEST, preferred_element_type=jnp.float32)


def normal_solve(pivot_block, right_side):
    gram = product(pivot_block.T, pivot_block)
    factor = jnp.linalg.cholesky(gram)
    return jax.scipy.linalg.cho_solve((factor, True), product(pivot_block.T, right_side))


def offset_in(first, anchor, extent, width):
    return jnp.clip(first - anchor, 0, extent - width)


def eliminate(matrix_tile, column_panel, first, row_index, width):
    row_count = matrix_tile.shape[0]
    owner_row = first // row_count
    row_offset = offset_in(first, row_index * row_count, row_count, width)
    own_rows = lax.dynamic_slice_in_dim(matrix_tile, row_offset, width, 0)
    local_block = lax.dynamic_slice_in_dim(column_panel, row_offset, width, 0)
    row_panel, pivot_block = (
        spread(own_rows, "row", owner_row),
        spread(local_block, "row", owner_row),
    )
    solved = normal_solve(pivot_block, row_panel)
    return matrix_tile - product(column_panel, solved)


def on_device(pivots, demand, prices):
    width = PW
    demand_rows = lax.all_gather(demand, "col", axis=1, tiled=True)
    price_columns = lax.all_gather(prices, "row", axis=0, tiled=True)
    row_count = demand_rows.shape[0]
    col_count = price_columns.shape[1]
    row_index = lax.axis_index("row")
    col_index = lax.axis_index("col")
    global_rows = row_index * row_count + jnp.arange(row_count, dtype=jnp.int32)
    global_cols = col_index * col_count + jnp.arange(col_count, dtype=jnp.int32)
    identity = (global_rows[:, None] == global_cols[None, :]).astype(jnp.float32)
    matrix_tile = identity - product(demand_rows, price_columns)
    first = pivots[0] * width
    second = pivots[1] * width
    owner_col = first // col_count
    col_offset = offset_in(first, col_index * col_count, col_count, width)
    column_panel = spread(
        lax.dynamic_slice_in_dim(matrix_tile, col_offset, width, 1), "col", owner_col
    )
    matrix_tile = eliminate(matrix_tile, column_panel, first, row_index, width)
    second_owner = second // col_count
    second_offset = offset_in(second, col_index * col_count, col_count, width)
    column_panel = spread(
        lax.dynamic_slice_in_dim(matrix_tile, second_offset, width, 1), "col", second_owner
    )
    return eliminate(matrix_tile, column_panel, second, row_index, width)


def solution(mesh):
    placed = (P(), P("row", "col"), P("row", "col"))
    return jax.shard_map(
        on_device, mesh=mesh, in_specs=placed, out_specs=P("row", "col"), check_vma=False
    )
```

profile of v0, /device:TPU:1, one launch (start us, length us, event | category | flops | bytes accessed | tf_op | source)
XLA Modules:
  0.0 862.2 jit_solution(7826932313319986005)
XLA Ops:
  6.5 0.7 all-gather.5.cloned.1.call-update
  7.3 0.7 all-gather.3.cloned.1.call-update
  8.1 1.3 fusion.32
  10.1 47.2 %all-gather.5.cloned.1.call-done = f32[512,512]{1,0:T(8,128)} async-done(((f32[32,512]{1,0:T(8,128)}), f32[512,512]{1,0:T(8,128)}) %all-gather.5.cloned.1.call-update) | async-done | bytes 1048592 | tf_op jit(solution)/shard_map/all_gather | solution.py:45
  57.2 79.4 %all-gather.3.cloned.1.call-done = f32[1024,512]{0,1:T(8,128)} async-done(((f32[1024,16]{0,1:T(8,128)}), f32[1024,512]{0,1:T(8,128)}) %all-gather.3.cloned.1.call-update) | async-done | bytes 2097168 | tf_op jit(solution)/shard_map/all_gather | solution.py:44
  136.6 5.5 convert_subtract_fusion
  142.1 1.3 dynamic-slice_select_fusion.1
  143.6 0.9 dynamic-slice_select_fusion.3
  144.5 157.7 %all-reduce.8.cloned.1.call-done = f32[1024,256]{1,0:T(8,128)} async-done(((f32[1024,256]{1,0:T(8,128)}), f32[1024,256]{1,0:T(8,128)}) %all-reduce.8.cloned.1.call-update) | async-done | bytes 1048592 | tf_op jit(solution)/shard_map/psum | solution.py:11
  302.2 1.7 dynamic-slice_select_fusion.5
  304.9 119.8 %all-reduce.14.cloned.1.call-done = (f32[256,256]{1,0:T(8,128)}, f32[256,512]{1,0:T(8,128)}) async-done(((f32[256,256]{1,0:T(8,128)}, f32[256,512]{1,0:T(8,128)}), (f32[256,256]{1,0:T(8,128)}, f32[256,512]{1,0:T(8,128)})) %all-reduce.14.cloned.1.call-update) | async-done | bytes 786448 | tf_op jit(solution)/shard_map/psum | solution.py:11
  424.7 1.6 fusion.33
  426.3 1.8 fusion.34
  428.3 11.7 %cholesky.130 = f32[128,128]{1,0:T(8,128)S(1)} custom-call(f32[128,128]{1,0:T(8,128)S(1)} %cholesky.194), custom_call_target="Cholesky" | custom-call | tf_op jit(solution)/shard_map/jit(cholesky)/cholesky | solution.py:20
  440.0 9.8 %custom-call.15 = f32[1,128,128]{1,2,0:T(8,128)S(1)} custom-call(f32[1,128,128]{2,1,0:T(8,128)S(1)} %get-tuple-element.54), custom_call_target="InvertDiagBlocksLowerTriangular" | custom-call | tf_op jit(solution)/shard_map/jit(cholesky)/cholesky | solution.py:20
  450.3 11.7 %cholesky.147 = f32[128,128]{1,0:T(8,128)S(1)} custom-call(f32[128,128]{1,0:T(8,128)S(1)} %convolution_subtract_fusion.7), custom_call_target="Cholesky" | custom-call | tf_op jit(solution)/shard_map/jit(cholesky)/cholesky | solution.py:20
  462.1 0.6 compare_reduce_fusion.2
  464.1 16.0 %while.4 = (s32[]{:T(128)}, f32[256,256]{1,0:T(8,128)S(1)}, s32[2,2]{1,0:T(2,128)S(1)}, f32[2,128,128]{2,1,0:T(8,128)S(1)}, s32[]{:T(128)}) while((s32[]{:T(128)}, f32[256,256]{1,0:T(8,128)S(1)}, s32[2,2]{1,0:T(2,128)S(1)}, f32[2,128,128]{2,1,0:T(8,128)S(1)}, s32[]{:T(128)}) %tuple.44), condition=%wide.while_cond, body=%wide.while_body.sunk | while | flops 2 | bytes 131189 | solution.py:21
  476.3 0.6 fusion.65
  476.9 1.3 bitcast_dynamic-update-slice_fusion.4
  478.2 0.6 fusion.65
  478.8 1.3 bitcast_dynamic-update-slice_fusion.4
  480.1 19.7 %custom-call.16 = f32[2,128,128]{1,2,0:T(8,128)S(1)} custom-call(f32[2,128,128]{2,1,0:T(8,128)S(1)} %get-tuple-element.21), custom_call_target="InvertDiagBlocksLowerTriangular" | custom-call | tf_op jit(solution)/shard_map/jit(_cho_solve)/triangular_solve | solution.py:21
  500.6 0.4 fusion.20
  501.4 0.4 convolution_subtract_fusion.4
  502.2 1.9 convolution_subtract_fusion.1
  504.1 1.3 copy-done
  505.4 1.4 dynamic-slice_select_fusion
  506.9 1.9 dynamic-slice_select_fusion.2
  508.8 154.4 %all-reduce.10.cloned.1.call-done = f32[1024,256]{1,0:T(8,128)} async-done(((f32[1024,256]{1,0:T(8,128)}), f32[1024,256]{1,0:T(8,128)}) %all-reduce.10.cloned.1.call-update) | async-done | bytes 1048592 | tf_op jit(solution)/shard_map/psum | solution.py:11
  663.2 1.7 dynamic-slice_select_fusion.4
  664.9 120.8 %all-reduce.12.cloned.1.call-done = (f32[256,256]{1,0:T(8,128)}, f32[256,512]{1,0:T(8,128)}) async-done(((f32[256,256]{1,0:T(8,128)}, f32[256,512]{1,0:T(8,128)}), (f32[256,256]{1,0:T(8,128)}, f32[256,512]{1,0:T(8,128)})) %all-reduce.12.cloned.1.call-update) | async-done | bytes 786448 | tf_op jit(solution)/shard_map/psum | solution.py:11
  785.7 1.6 fusion.35
  787.3 1.7 fusion.36
  789.3 11.7 %cholesky.164 = f32[128,128]{1,0:T(8,128)S(1)} custom-call(f32[128,128]{1,0:T(8,128)S(1)} %cholesky.197), custom_call_target="Cholesky" | custom-call | tf_op jit(solution)/shard_map/jit(cholesky)/cholesky | solution.py:20
  801.1 9.8 %custom-call.17 = f32[1,128,128]{1,2,0:T(8,128)S(1)} custom-call(f32[1,128,128]{2,1,0:T(8,128)S(1)} %get-tuple-element.50), custom_call_target="InvertDiagBlocksLowerTriangular" | custom-call | tf_op jit(solution)/shard_map/jit(cholesky)/cholesky | solution.py:20
  811.4 11.7 %cholesky.181 = f32[128,128]{1,0:T(8,128)S(1)} custom-call(f32[128,128]{1,0:T(8,128)S(1)} %convolution_subtract_fusion.6), custom_call_target="Cholesky" | custom-call | tf_op jit(solution)/shard_map/jit(cholesky)/cholesky | solution.py:20
  823.1 0.7 compare_reduce_fusion.1
  823.8 0.6 compare_reduce_fusion
  825.7 4.1 while.5
  825.9 0.6 fusion.66
  826.5 1.3 bitcast_dynamic-update-slice_fusion.5
  827.9 0.6 fusion.66
  828.5 1.3 bitcast_dynamic-update-slice_fusion.5
  829.8 19.7 %custom-call.18 = f32[2,128,128]{1,2,0:T(8,128)S(1)} custom-call(f32[2,128,128]{2,1,0:T(8,128)S(1)} %get-tuple-element.22), custom_call_target="InvertDiagBlocksLowerTriangular" | custom-call | tf_op jit(solution)/shard_map/jit(_cho_solve)/triangular_solve | solution.py:21
  850.3 0.4 fusion.23
  851.1 0.4 convolution_subtract_fusion.2
  852.0 3.2 convolution_subtract_fusion
  (53 shorter events, 5.4 us)
Async XLA Ops:
  6.5 50.7 %all-gather.5.cloned.1.call-start = ((), (), s32[]{:S(2)}) async-start(), calls=%async_computation.1 | async-start | bytes 1114112 | tf_op jit(solution)/shard_map/all_gather | solution.py:45
  7.3 129.4 %all-gather.3.cloned.1.call-start = ((), (), s32[]{:S(2)}) async-start(), calls=%async_computation | async-start | bytes 2162688 | tf_op jit(solution)/shard_map/all_gather | solution.py:44
  8.0 294.2 %all-reduce.8.cloned.1.call-start = ((), (), s32[]{:S(2)}) async-start(), calls=%async_computation.2 | async-start | bytes 2097152 | tf_op jit(solution)/shard_map/psum | solution.py:11
  143.5 281.2 %all-reduce.14.cloned.1.call-start = ((), (), s32[]{:S(2)}) async-start(), calls=%async_computation.5 | async-start | bytes 1572864 | tf_op jit(solution)/shard_map/psum | solution.py:11
  303.9 359.3 %all-reduce.10.cloned.1.call-start = ((), (), s32[]{:S(2)}) async-start(), calls=%async_computation.3 | async-start | bytes 2097152 | tf_op jit(solution)/shard_map/psum | solution.py:11
  499.8 2.4 copy-start.2
  504.1 1.3 copy-start
  506.8 278.9 %all-reduce.12.cloned.1.call-start = ((), (), s32[]{:S(2)}) async-start(), calls=%async_computation.4 | async-start | bytes 1572864 | tf_op jit(solution)/shard_map/psum | solution.py:11
  829.8 22.1 %copy-start.1 = (f32[1024,512]{1,0:T(8,128)S(1)}, f32[1024,512]{1,0:T(8,128)}, u32[]{:S(2)}) copy-start(f32[1024,512]{1,0:T(8,128)} %copy-done) | copy-start | bytes 6291460
  849.5 2.4 copy-start.3
Sparse Core Ops, SparseCore 0:
  9.4 47.7 all-gather.4
  60.4 76.1 all-gather.2
  143.6 158.5 all-reduce.7
  304.5 120.1 all-reduce.13
  506.9 156.2 all-reduce.9
  665.5 120.1 all-reduce.11
where the time goes:
time: 866 us; the launch traced here: 862 us
  waiting for transfers between devices  681 us (79%)
  other arithmetic  117 us (14%)
  matrix products  23 us (3%)
  between operations  17.8 us (2%)
  loops' own time  12.5 us (1%)
  local copies, waits for them, and re-layouts  10.7 us (1%)
    psum x4, waiting for transfers between devices, spread(): return lax.psum(block, axis)  553 us
    all_gather x1, waiting for transfers between devices, on_device(): demand_rows = lax.all_gather(demand, 'col', axis=1, tiled=True)  79.4 us
    another operation x13, other arithmetic, normal_solve(): factor = jnp.linalg.cholesky(gram)  68.6 us
    all_gather x1, waiting for transfers between devices, on_device(): price_columns = lax.all_gather(prices, 'row', axis=0, tiled=True)  47.2 us
    another operation x5, other arithmetic, normal_solve(): jax.scipy.linalg.cho_solve((factor, True), product(pivot_block.T, right_s...  39.4 us
  transfers between devices with their start and end apart: 6, of which 6 were waited for; matrix products, arithmetic and copies ran while one was open for 0% of the time, Pallas kernels for 0%

commit v1 on v0

--- a/solution.py
+++ b/solution.py
@@ -8,7 +8,7 @@
 
 def spread(block, axis, holder):
     block = jnp.where(lax.axis_index(axis) == holder, block, jnp.zeros_like(block))
-    return lax.psum(block, axis)
+    return jnp.sum(lax.all_gather(block, axis), axis=0)
 
 
 def product(left, right):

time: 866 us -> 997 us (1.15)
  waiting for transfers between devices: 681 us -> 774 us
  other arithmetic: 117 us -> 158 us
  loops' own time: 12.5 us -> 0.1 us
    all_gather x0 -> x6, waiting for transfers between devices: none -> 646 us  [spread(): return jnp.sum(lax.all_gather(block, axis), axis=0)]
    psum x4 -> x0, waiting for transfers between devices: 553 us -> none  [spread(): return lax.psum(block, axis)]
    reduce_sum x0 -> x6, other arithmetic: none -> 38.6 us  [spread(): return jnp.sum(lax.all_gather(block, axis), axis=0)]
    another operation x2, loops' own time: 12.5 us -> 0.1 us  [normal_solve(): jax.scipy.linalg.cho_solve((factor, True), product(pivot_block.T, right_s...]
  transfers between devices with their start and end apart: 6 -> 8, of which waited for: 6 -> 8; matrix products, arithmetic and copies ran while one was open for 0% -> 4% of each run, Pallas kernels for 0% -> 0%
where the time goes in v1:
time: 997 us; the launch traced here: 992 us
  waiting for transfers between devices  774 us (78%)
  other arithmetic  158 us (16%)
  matrix products  24.4 us (2%)
  between operations  18 us (2%)
  local copies, waits for them, and re-layouts  16.5 us (2%)
    all_gather x6, waiting for transfers between devices, spread(): return jnp.sum(lax.all_gather(block, axis), axis=0)  646 us
    all_gather x1, waiting for transfers between devices, on_device(): demand_rows = lax.all_gather(demand, 'col', axis=1, tiled=True)  79.4 us
    another operation x13, other arithmetic, normal_solve(): factor = jnp.linalg.cholesky(gram)  69.6 us
    all_gather x1, waiting for transfers between devices, on_device(): price_columns = lax.all_gather(prices, 'row', axis=0, tiled=True)  47.1 us
    another operation x5, other arithmetic, normal_solve(): jax.scipy.linalg.cho_solve((factor, True), product(pivot_block.T, right_s...  41.9 us
    reduce_sum x6, other arithmetic, spread(): return jnp.sum(lax.all_gather(block, axis), axis=0)  38.6 us
  transfers between devices with their start and end apart: 8, of which 8 were waited for; matrix products, arithmetic and copies ran while one was open for 4% of the time, Pallas kernels for 0%

profile of v1, /device:TPU:1, one launch (start us, length us, event | category | flops | bytes accessed | tf_op | source)
XLA Modules:
  0.0 991.6 jit_solution(15497584950440489017)
XLA Ops:
  8.1 1.4 fusion.32
  10.1 47.1 %all-gather.17.cloned.1.call-done = f32[512,512]{1,0:T(8,128)} async-done(((f32[32,512]{1,0:T(8,128)}), f32[512,512]{1,0:T(8,128)}) %all-gather.17.cloned.1.call-update) | async-done | bytes 1048592 | tf_op jit(solution)/shard_map/all_gather | solution.py:45
  57.2 79.4 %all-gather.15.cloned.1.call-done = f32[1024,512]{0,1:T(8,128)} async-done(((f32[1024,16]{0,1:T(8,128)}), f32[1024,512]{0,1:T(8,128)}) %all-gather.15.cloned.1.call-update) | async-done | bytes 2097168 | tf_op jit(solution)/shard_map/all_gather | solution.py:44
  136.6 5.5 convert_subtract_fusion
  142.1 1.3 dynamic-slice_select_fusion.1
  143.6 0.9 dynamic-slice_select_fusion.3
  144.5 238.5 %all-gather.19.cloned.1.call-done = f32[32768,256]{1,0:T(8,128)} async-done(((f32[1024,256]{1,0:T(8,128)}), f32[32768,256]{1,0:T(8,128)}) %all-gather.19.cloned.1.call-update) | async-done | bytes 33554448 | tf_op jit(solution)/shard_map/all_gather | solution.py:11
  383.0 11.9 %reduce_sum.54 = f32[1024,256]{1,0:T(8,128)S(1)} reduce(f32[32,1024,256]{2,1,0:T(8,128)} %bitcast.93, f32[]{:T(128)} %constant.129.clone.1), dimensions={0}, to_apply=%region_0.1 | reduce | flops 8126464 | bytes 34603012 | tf_op jit(solution)/shard_map/reduce_sum | solution.py:11
  395.0 0.7 dynamic-slice_select_fusion.5
  397.0 46.0 %all-gather.23.cloned.1.call-done = f32[4096,512]{1,0:T(8,128)} async-done(((f32[256,512]{1,0:T(8,128)}), f32[4096,512]{1,0:T(8,128)}) %all-gather.23.cloned.1.call-update) | async-done | bytes 8388624 | tf_op jit(solution)/shard_map/all_gather | solution.py:11
  443.0 5.2 reduce_sum.56
  448.2 40.0 %all-gather.21.cloned.1.call-done = f32[4096,256]{1,0:T(8,128)} async-done(((f32[256,256]{1,0:T(8,128)}), f32[4096,256]{1,0:T(8,128)}) %all-gather.21.cloned.1.call-update) | async-done | bytes 4194320 | tf_op jit(solution)/shard_map/all_gather | solution.py:11
  488.2 2.5 reduce_sum.55
  490.6 1.3 fusion.33
  491.9 1.8 copy.6
  493.7 1.1 fusion.11
  495.5 11.7 %cholesky.130 = f32[128,128]{1,0:T(8,128)S(1)} custom-call(f32[128,128]{1,0:T(8,128)S(1)} %cholesky.194), custom_call_target="Cholesky" | custom-call | tf_op jit(solution)/shard_map/jit(cholesky)/cholesky | solution.py:20
  507.9 9.8 custom-call.15
  517.8 1.7 constant_dynamic-update-slice_fusion.1
  519.4 1.1 convolution_subtract_fusion.7
  520.5 11.9 %cholesky.147 = f32[128,128]{1,0:T(8,128)S(1)} custom-call(f32[128,128]{1,0:T(8,128)S(1)} %convolution_subtract_fusion.7), custom_call_target="Cholesky" | custom-call | tf_op jit(solution)/shard_map/jit(cholesky)/cholesky | solution.py:20
  535.0 1.7 select_select_fusion.1
  536.8 5.8 while.4
  537.4 2.2 bitcast_dynamic-update-slice_fusion.4
  540.3 2.2 bitcast_dynamic-update-slice_fusion.4
  543.2 20.5 %custom-call.16 = f32[2,128,128]{1,2,0:T(8,128)S(1)} custom-call(f32[2,128,128]{2,1,0:T(8,128)} %copy-done.3), custom_call_target="InvertDiagBlocksLowerTriangular" | custom-call | tf_op jit(solution)/shard_map/jit(_cho_solve)/triangular_solve | solution.py:21
  563.7 1.7 fusion.34
  565.8 1.2 convolution_subtract_fusion.5
  567.8 1.3 convolution_subtract_fusion.4
  569.4 1.9 convolution_subtract_fusion.1
  571.3 1.3 copy-done
  572.7 1.3 dynamic-slice_select_fusion
  574.1 1.9 dynamic-slice_select_fusion.2
  576.1 233.0 %all-gather.25.cloned.1.call-done = f32[32768,256]{1,0:T(8,128)} async-done(((f32[1024,256]{1,0:T(8,128)}), f32[32768,256]{1,0:T(8,128)}) %all-gather.25.cloned.1.call-update) | async-done | bytes 33554448 | tf_op jit(solution)/shard_map/all_gather | solution.py:11
  809.0 12.1 %reduce_sum.57 = f32[1024,256]{1,0:T(8,128)S(1)} reduce(f32[32,1024,256]{2,1,0:T(8,128)} %bitcast.92, f32[]{:T(128)} %constant.129.clone.1), dimensions={0}, to_apply=%region_7.10 | reduce | flops 8126464 | bytes 34603012 | tf_op jit(solution)/shard_map/reduce_sum | solution.py:11
  821.2 0.7 dynamic-slice_select_fusion.4
  822.0 47.2 %all-gather.29.cloned.1.call-done = f32[4096,512]{1,0:T(8,128)} async-done(((f32[256,512]{1,0:T(8,128)}), f32[4096,512]{1,0:T(8,128)}) %all-gather.29.cloned.1.call-update) | async-done | bytes 8388624 | tf_op jit(solution)/shard_map/all_gather | solution.py:11
  869.1 4.4 reduce_sum.59
  873.5 40.9 %all-gather.27.cloned.1.call-done = f32[4096,256]{1,0:T(8,128)} async-done(((f32[256,256]{1,0:T(8,128)}), f32[4096,256]{1,0:T(8,128)}) %all-gather.27.cloned.1.call-update) | async-done | bytes 4194320 | tf_op jit(solution)/shard_map/all_gather | solution.py:11
  914.5 2.5 reduce_sum.58
  917.8 11.7 %cholesky.164 = f32[128,128]{1,0:T(8,128)S(1)} custom-call(f32[128,128]{1,0:T(8,128)S(1)} %cholesky.197), custom_call_target="Cholesky" | custom-call | tf_op jit(solution)/shard_map/jit(cholesky)/cholesky | solution.py:20
  929.5 9.8 custom-call.17
  939.8 11.9 %cholesky.181 = f32[128,128]{1,0:T(8,128)S(1)} custom-call(f32[128,128]{1,0:T(8,128)S(1)} %convolution_subtract_fusion.6), custom_call_target="Cholesky" | custom-call | tf_op jit(solution)/shard_map/jit(cholesky)/cholesky | solution.py:20
  954.4 4.1 while.5
  955.1 1.3 bitcast_dynamic-update-slice_fusion.5
  957.2 1.3 bitcast_dynamic-update-slice_fusion.5
  958.5 19.7 %custom-call.18 = f32[2,128,128]{1,2,0:T(8,128)S(1)} custom-call(f32[2,128,128]{2,1,0:T(8,128)S(1)} %get-tuple-element.22), custom_call_target="InvertDiagBlocksLowerTriangular" | custom-call | tf_op jit(solution)/shard_map/jit(_cho_solve)/triangular_solve | solution.py:21
  981.3 3.2 convolution_subtract_fusion
  (65 shorter events, 15.8 us)
Async XLA Ops:
  6.5 50.7 %all-gather.17.cloned.1.call-start = ((), (), s32[]{:S(2)}) async-start(), calls=%async_computation.1 | async-start | bytes 1114112 | tf_op jit(solution)/shard_map/all_gather | solution.py:45
  7.3 129.4 %all-gather.15.cloned.1.call-start = ((), (), s32[]{:S(2)}) async-start(), calls=%async_computation | async-start | bytes 2162688 | tf_op jit(solution)/shard_map/all_gather | solution.py:44
  8.0 375.0 %all-gather.19.cloned.1.call-start = ((), (), s32[]{:S(2)}) async-start(), calls=%async_computation.2 | async-start | bytes 34603008 | tf_op jit(solution)/shard_map/all_gather | solution.py:11
  143.5 299.5 %all-gather.23.cloned.1.call-start = ((), (), s32[]{:S(2)}) async-start(), calls=%async_computation.4 | async-start | bytes 8912896 | tf_op jit(solution)/shard_map/all_gather | solution.py:11
  144.5 343.7 %all-gather.21.cloned.1.call-start = ((), (), s32[]{:S(2)}) async-start(), calls=%async_computation.3 | async-start | bytes 4456448 | tf_op jit(solution)/shard_map/all_gather | solution.py:11
  395.7 413.3 %all-gather.25.cloned.1.call-start = ((), (), s32[]{:S(2)}) async-start(), calls=%async_computation.5 | async-start | bytes 34603008 | tf_op jit(solution)/shard_map/all_gather | solution.py:11
  494.8 0.7 copy-start.2
  542.5 0.7 copy-start.3
  571.3 1.3 copy-start
  574.0 295.1 %all-gather.29.cloned.1.call-start = ((), (), s32[]{:S(2)}) async-start(), calls=%async_computation.7 | async-start | bytes 8912896 | tf_op jit(solution)/shard_map/all_gather | solution.py:11
  576.0 338.4 %all-gather.27.cloned.1.call-start = ((), (), s32[]{:S(2)}) async-start(), calls=%async_computation.6 | async-start | bytes 4456448 | tf_op jit(solution)/shard_map/all_gather | solution.py:11
  978.8 2.4 copy-start.1
Sparse Core Ops, SparseCore 0:
  9.4 47.7 all-gather.16
  60.4 76.1 all-gather.14
  143.6 239.3 all-gather.18
  385.0 57.9 all-gather.22
  444.9 43.1 all-gather.20
  574.1 234.8 all-gather.24
  811.2 57.9 all-gather.28
  871.3 43.1 all-gather.26
